TPU v7x, 128 devices: a whole 4x4x4 slice. The times are simulated.
128 devices in a mesh: row: 8 (over y, core), col: 16 (over x, z).
Axes of the slice: x: 4, y: 4, z: 4, core: 2. Of those that a mesh axis runs over, the one named last changes fastest.
Arguments:
- valence_bands: bfloat16 [256, 96, 9216], P(('row', 'col')), may hold values from -6 to 6
- conduction_bands: bfloat16 [256, 96, 9216], P(('row', 'col')), may hold values from -6 to 6
- valence_energy: float32 [256], P(('row', 'col')), may hold values from -8 to -0.5
- conduction_energy: float32 [256], P(('row', 'col')), may hold values from 0.5 to 8
- pair_valence: int32 [128, 4], P(('row', 'col')), may hold values from 0 to 1
- pair_conduction: int32 [128, 4], P(('row', 'col')), may hold values from 0 to 1
- pair_count: int32 [128], replicated, may hold values from 1 to 4, 256 in all
- stick_perm: int32 [160], replicated, may hold values from 0 to 159, each once
Outputs:
- response: float32 [20480, 20480], P('row', 'col')
Inputs may be any that keep to these rules, and one draw needn't show every extreme that they name: `pair_count`: the numbers sum to 256 and the largest is 4. `stick_perm`: A permutation of the box sticks.
All inputs are finite; a program needn't handle non-finite values.
Results may differ from a plain program's by a relative error of at most 0.0003.
Values sent between devices are 32-bit elements; how exact they have to be, the bound alone decides.
No kernel may reach another device: no remote copies, remote signals or barrier semaphores. Data moves between devices by JAX's collectives and lax.ppermute only.
A program may use at most 128 MiB of HBM per device.

v0:
```python
import math
import jax
import jax.numpy as jnp
from jax import lax
from jax.sharding import PartitionSpec as P

KX = 10
KY = 16
KZ = 64
CAP = 4
NPW = 20480


def transform(product):
    grid_size = product.shape[1]
    position = jnp.arange(grid_size, dtype=jnp.int32)

    def phases(frequency):
        return (frequency[:, None] * position[None, :] % grid_size).astype(jnp.float32) * (
            2.0 * math.pi / grid_size
        )

    x_phase = phases(jnp.arange(1, KX + 1, dtype=jnp.int32))
    y_phase = phases(jnp.arange(KY, dtype=jnp.int32))
    z_phase = phases(jnp.arange(KZ, dtype=jnp.int32))
    x_factor = jnp.concatenate([jnp.cos(x_phase), -jnp.sin(x_phase)], axis=0)
    x_section = jnp.einsum("gx,kxp->kgp", x_factor, product, precision=lax.Precision.HIGHEST)
    x_section = x_section.reshape(product.shape[0], 2 * KX, grid_size, grid_size)
    x_real = x_section[:, :KX]
    x_imag = x_section[:, KX:]
    y_cosine = jnp.cos(y_phase)
    y_sine = jnp.sin(y_phase)

    def along_y(factor_table, operand):
        return jnp.einsum("hy,kgyz->kghz", factor_table, operand, precision=lax.Precision.HIGHEST)

    y_real = along_y(y_cosine, x_real) + along_y(y_sine, x_imag)
    y_imag = along_y(y_cosine, x_imag) - along_y(y_sine, x_real)
    z_cosine = jnp.cos(z_phase).T
    z_sine = jnp.sin(z_phase).T

    def along_z(factor_table, operand):
        return jnp.einsum("kghz,zm->kghm", operand, factor_table, precision=lax.Precision.HIGHEST)

    z_real = along_z(z_cosine, y_real) + along_z(z_sine, y_imag)
    z_imag = along_z(z_cosine, y_imag) - along_z(z_sine, y_real)
    sticks = jnp.concatenate([z_real, z_imag], axis=-1) * grid_size ** (-1.5)
    return sticks.reshape(product.shape[0], KX * KY, 2 * KZ)


def body(
    valence_bands,
    conduction_bands,
    valence_energy,
    conduction_energy,
    pair_valence,
    pair_conduction,
    pair_count,
    stick_perm,
):
    row_devices = lax.axis_size("row")
    column_devices = lax.axis_size("col")
    devices = row_devices * column_devices
    self_index = lax.axis_index("row") * column_devices + lax.axis_index("col")
    slot_valence = pair_valence[0]
    slot_conduction = pair_conduction[0]
    live_slots = jnp.arange(CAP, dtype=jnp.int32) < pair_count[self_index]
    left_band = jnp.take(valence_bands, slot_valence, axis=0)
    right_band = jnp.take(conduction_bands, slot_conduction, axis=0)
    product = left_band.astype(jnp.float32) * right_band.astype(jnp.float32)
    sticks = transform(product)
    density = jnp.take(sticks, stick_perm, axis=1).reshape(CAP, NPW)
    weight = -1.0 / (
        jnp.take(conduction_energy, slot_conduction) - jnp.take(valence_energy, slot_valence)
    )
    weight = jnp.where(live_slots, weight, 0.0)
    weighted = density * weight[:, None]
    owned_width = NPW // devices
    row_side = weighted.reshape(CAP, devices, owned_width)
    column_side = (
        density.reshape(CAP, column_devices, row_devices, owned_width)
        .transpose(0, 2, 1, 3)
        .reshape(CAP, devices, owned_width)
    )
    row_pieces, column_pieces = (
        lax.all_to_all(row_side, ("row", "col"), split_axis=1, concat_axis=1, tiled=True),
        lax.all_to_all(column_side, ("row", "col"), split_axis=1, concat_axis=1, tiled=True),
    )
    row_received = row_pieces.reshape(CAP * devices, owned_width)
    column_received = column_pieces.reshape(CAP * devices, owned_width)
    column_panel = lax.all_gather(column_received, "row", axis=1, tiled=True)
    return lax.dot_general(
        lax.all_gather(row_received, "col", axis=1, tiled=True),
        column_panel,
        (((0,), (0,)), ((), ())),
        precision=lax.Precision.HIGHEST,
        preferred_element_type=jnp.float32,
    )


def solution(mesh):
    return jax.shard_map(
        body,
        mesh=mesh,
        in_specs=(
            P(("row", "col"), None, None),
            P(("row", "col"), None, None),
            P(("row", "col")),
            P(("row", "col")),
            P(("row", "col"), None),
            P(("row", "col"), None),
            P(),
            P(),
        ),
        out_specs=P("row", "col"),
        check_vma=False,
    )
```

profile of v0, /device:TPU:1, one launch (start us, length us, event | category | flops | bytes accessed | tf_op | source)
XLA Modules:
  0.0 219.2 jit_solution(10084126790357145682)
XLA Ops:
  6.5 1.4 compare_and_fusion.2
  8.0 1.3 compare_select_fusion
  10.6 1.3 compare_and_fusion
  13.1 4.0 %gather_fusion.1 = bf16[4,96,9216]{2,1,0:T(8,128)(2,1)} fusion(bf16[2,96,9216]{2,1,0:T(8,128)(2,1)S(1)} %copy-done, s32[1024]{0:T(1024)} %pad_clamp_fusion.2), kind=kCustom, calls=%fused_computation.clone | custom fusion | bytes 14155792 | tf_op jit(solution)/shard_map/jit(_take)/gather | solution.py:68
  17.2 6.1 %gather_fusion.2 = bf16[4,96,9216]{2,1,0:T(8,128)(2,1)} fusion(bf16[2,96,9216]{2,1,0:T(8,128)(2,1)} %param.13, s32[1024]{0:T(1024)} %pad_clamp_fusion.1), kind=kCustom, calls=%fused_computation.2.clone | custom fusion | bytes 14155792 | tf_op jit(solution)/shard_map/jit(_take)/gather | solution.py:69
  23.2 13.6 %fusion.4 = f32[4,20,9216]{2,1,0:T(8,128)} fusion(bf16[4,96,9216]{2,1,0:T(8,128)(2,1)} %gather_fusion.2, bf16[4,96,9216]{2,1,0:T(8,128)(2,1)} %gather_fusion.1, pred[4]{0:T(512)(128)(4,1)} %get-tuple-element.9, pred[4]{0:T(512)(128)(4,1)} %get-tuple-element.10, f32[10,96]{1,0:T(8,128)S(1)} %get-tuple-element.8, f32[10,96]{1,0:T(8,128)S(1)} %get-tuple-element.6), kind=kOutput, calls=%fused_computation.9 | convolution fusion | flops 867043200 | bytes 17112584 | tf_op jit(solution)/shard_map/gx,kxp->kgp/dot_general | solution.py:27
  36.8 4.3 %reshape.114 = f32[4,20,96,96]{3,2,1,0:T(8,128)} reshape(f32[4,20,9216]{2,1,0:T(8,128)} %fusion.4) | data formatting | bytes 5898240 | tf_op jit(solution)/shard_map/reshape | solution.py:28
  41.1 3.4 %fusion.53 = f32[4,10,96,16]{2,3,1,0:T(8,128)} fusion(f32[4,20,96,96]{3,2,1,0:T(8,128)} %reshape.114), kind=kOutput, calls=%fused_computation.62 | convolution fusion | flops 70792704 | bytes 3194880 | tf_op jit(solution)/shard_map/hy,kgyz->kghz/dot_general | solution.py:35
  44.6 3.4 %fusion.51 = f32[4,10,96,16]{2,3,1,0:T(8,128)} fusion(f32[4,20,96,96]{3,2,1,0:T(8,128)} %reshape.114), kind=kOutput, calls=%fused_computation.60 | convolution fusion | flops 70792704 | bytes 3194880 | tf_op jit(solution)/shard_map/hy,kgyz->kghz/dot_general | solution.py:35
  48.7 1.5 broadcast_in_dim.51
  50.2 2.7 %fusion.13 = f32[4,10,16,96]{3,2,1,0:T(8,128)S(1)} fusion(f32[4,10,96,16]{2,3,1,0:T(8,128)} %fusion.53, f32[4,20,96,96]{3,2,1,0:T(8,128)} %reshape.114), kind=kOutput, calls=%fused_computation.20 | convolution fusion | flops 70854144 | bytes 3440640 | tf_op jit(solution)/shard_map/hy,kgyz->kghz/dot_general | solution.py:35
  53.5 2.7 %fusion.12 = f32[4,10,16,96]{3,2,1,0:T(8,128)S(1)} fusion(f32[4,10,96,16]{2,3,1,0:T(8,128)} %fusion.51, f32[4,20,96,96]{3,2,1,0:T(8,128)} %reshape.114), kind=kOutput, calls=%fused_computation.18 | convolution fusion | flops 70854144 | bytes 3440640 | tf_op jit(solution)/shard_map/hy,kgyz->kghz/dot_general | solution.py:35
  59.3 2.5 %gather_fusion = f32[160,4,128]{2,1,0:T(4,128)} fusion(f32[4,160,128]{2,0,1:T(4,128)} %maximum_multiply_fusion, s32[1024]{0:T(1024)S(1)} %pad_clamp_fusion), kind=kCustom, calls=%fused_computation.4 | custom fusion | bytes 656000 | tf_op jit(solution)/shard_map/jit(_take)/gather | solution.py:72
  61.9 1.7 copy.52
  63.6 2.0 gather.16
  67.2 24.8 %all_to_all.10 = f32[4,128,160]{2,0,1:T(4,128)} all-to-all(f32[4,128,160]{2,0,1:T(4,128)S(1)} %copy.58), channel_id=1, replica_groups=mesh['row'=8,'col'=16] {'row','col'}, dimensions={1} | all-to-all | bytes 655360 | tf_op jit(solution)/shard_map/all_to_all | solution.py:87
  92.0 2.0 copy.59
  94.0 1.7 copy.69
  95.8 1.5 broadcast_in_dim.46
  97.3 2.0 gather.15
  99.3 1.3 gather_fusion.3
  101.3 1.5 copy.46
  102.8 2.0 copy.53
  104.8 1.2 dynamic_slice.3
  106.0 1.3 compare_select_fusion.3
  107.3 1.8 select_multiply_fusion
  109.1 2.0 copy.54
  111.1 19.1 %all_to_all.11 = f32[4,128,160]{2,0,1:T(4,128)} all-to-all(f32[4,128,160]{2,0,1:T(4,128)} %copy.54), channel_id=1, replica_groups=mesh['row'=8,'col'=16] {'row','col'}, dimensions={1} | all-to-all | bytes 655360 | tf_op jit(solution)/shard_map/all_to_all | solution.py:86
  130.2 2.0 copy.55
  132.2 1.8 copy.70
  134.0 52.6 %all-gather.3.cloned.1.call-done = f32[512,2560]{0,1:T(8,128)} async-done(((f32[512,160]{0,1:T(8,128)}), f32[512,2560]{0,1:T(8,128)}) %all-gather.3.cloned.1.call-update) | async-done | bytes 5242896 | tf_op jit(solution)/shard_map/all_gather | solution.py:93
  186.5 25.8 %fusion.106 = f32[2560,1280]{1,0:T(8,128)} fusion(f32[512,2560]{0,1:T(8,128)} %all-gather.3.cloned.1.call-done, f32[512,1280]{0,1:T(8,128)} %all-gather.5.cloned.1.call-done), kind=kOutput, calls=%fused_computation.122 | convolution fusion | flops 20132659200 | bytes 20971520 | tf_op jit(solution)/shard_map/dot_general | solution.py:92
  (38 shorter events, 9.4 us)
Async XLA Ops:
  6.5 6.6 %copy-start = (bf16[2,96,9216]{2,1,0:T(8,128)(2,1)S(1)}, bf16[2,96,9216]{2,1,0:T(8,128)(2,1)}, u32[]{:S(2)}) copy-start(bf16[2,96,9216]{2,1,0:T(8,128)(2,1)} %param.12) | copy-start | bytes 10616836
  6.5 127.4 %all-gather.5.cloned.1.call-start = ((), (), s32[]{:S(2)}) async-start(), calls=%async_computation.3 | async-start | bytes 2949120 | tf_op jit(solution)/shard_map/all_gather | solution.py:91
  36.8 11.2 %copy-start.3 = (s32[160]{0:T(256)S(1)}, s32[160]{0:T(256)}, u32[]{:S(2)}) copy-start(s32[160]{0:T(256)} %compare_select_fusion) | copy-start | bytes 1924
  36.8 11.2 %copy-start.6 = (pred[160]{0:T(512)(128)(4,1)S(1)}, pred[160]{0:T(512)(128)(4,1)}, u32[]{:S(2)}) copy-start(pred[160]{0:T(512)(128)(4,1)} %compare_and_fusion.2) | copy-start | bytes 484
  58.1 41.2 %copy-start.1 = (f32[2]{0:T(128)S(1)}, f32[2]{0:T(128)}, u32[]{:S(2)}) copy-start(f32[2]{0:T(128)} %param.15) | copy-start | bytes 28
  58.3 42.3 %copy-start.2 = (f32[2]{0:T(128)S(1)}, f32[2]{0:T(128)}, u32[]{:S(2)}) copy-start(f32[2]{0:T(128)} %param.14) | copy-start | bytes 28
  61.8 44.2 %copy-start.4 = (s32[1,4]{1,0:T(1,128)S(1)}, s32[1,4]{1,0:T(1,128)}, u32[]{:S(2)}) copy-start(s32[1,4]{1,0:T(1,128)} %param.17) | copy-start | bytes 52
  61.9 44.2 %copy-start.5 = (s32[1,4]{1,0:T(1,128)S(1)}, s32[1,4]{1,0:T(1,128)}, u32[]{:S(2)}) copy-start(s32[1,4]{1,0:T(1,128)} %param.16) | copy-start | bytes 52
  95.8 90.8 %all-gather.3.cloned.1.call-start = ((), (), s32[]{:S(2)}) async-start(), calls=%async_computation.2 | async-start | bytes 5570560 | tf_op jit(solution)/shard_map/all_gather | solution.py:93
Sparse Core Ops, SparseCore 0:
  95.9 22.6 all-gather.4
  134.0 52.4 all-gather.2
where the time goes:
time: 220 us; the launch traced here: 219 us
  matrix products  53.9 us (24%)
  waiting for transfers between devices  52.6 us (24%)
  blocking collectives  44 us (20%)
  local copies, waits for them, and re-layouts  43.4 us (20%)
  between operations  13.5 us (6%)
  other arithmetic  11.7 us (5%)
    all_gather x1, waiting for transfers between devices, body(): lax.all_gather(row_received, 'col', axis=1, tiled=True)  52.6 us
    dot_general x1, matrix products, body(): lax.dot_general(lax.all_gather(row_received, 'col', axis=1, tiled=True),...  25.8 us
    all_to_all x1, blocking collectives, body(): lax.all_to_all(column_side, ('row', 'col'), split_axis=1, concat_axis=1,...  24.8 us
    all_to_all x1, blocking collectives, body(): lax.all_to_all(row_side, ('row', 'col'), split_axis=1, concat_axis=1, til...  19.1 us
    dot_general x1, matrix products, transform(): jnp.einsum('gx,kxp->kgp', x_factor, product, precision=lax.Precision.HIGH...  13.6 us
    dot_general x4, matrix products, along_y(): jnp.einsum('hy,kgyz->kghz', factor_table, operand, precision=lax.Precisio...  12.3 us
    gather x5, local copies, waits for them, and re-layouts, body(): density = jnp.take(sticks, stick_perm, axis=1).reshape(CAP, NPW)  10.3 us
    gather x1, local copies, waits for them, and re-layouts, body(): right_band = jnp.take(conduction_bands, slot_conduction, axis=0)  6.08 us
  transfers between devices with their start and end apart: 2, of which 1 were waited for; matrix products, arithmetic and copies ran while one was open for 9% of the time, Pallas kernels for 0%

commit v1 on v0

--- a/solution.py
+++ b/solution.py
@@ -90,7 +90,9 @@
     column_received = column_pieces.reshape(CAP * devices, owned_width)
     column_panel = lax.all_gather(column_received, "row", axis=1, tiled=True)
     return lax.dot_general(
-        lax.all_gather(row_received, "col", axis=1, tiled=True),
+        jnp.concatenate(
+            lax.all_to_all(jnp.stack([row_received] * lax.axis_size("col")), "col", 0, 0), axis=1
+        ),
         column_panel,
         (((0,), (0,)), ((), ())),
         precision=lax.Precision.HIGHEST,

time: 220 us -> 247 us (1.12); the launches traced: 219 us -> 243 us
  blocking collectives: 44 us -> 0 us
  waiting for transfers between devices: 52.6 us -> 92.2 us
  starting transfers between devices: 0.04 us -> 22.4 us
  local copies, waits for them, and re-layouts: 43.4 us -> 48.9 us
    all_to_all x0 -> x3, waiting for transfers between devices: none -> 65.6 us  [the longest x1 48.9 us: body(): lax.all_to_all(jnp.stack([row_received] * lax.axis_size('col')), 'col', 0...]
    all_gather x1 -> x0, waiting for transfers between devices: 52.6 us -> none  [body(): lax.all_gather(row_received, 'col', axis=1, tiled=True)]
    all_to_all x2 -> x0, blocking collectives: 44 us -> none  [the longest x1 24.8 us: body(): lax.all_to_all(column_side, ('row', 'col'), split_axis=1, concat_axis=1,...]
    all_gather x1, waiting for transfers between devices: 0.02 us -> 26.6 us  [body(): column_panel = lax.all_gather(column_received, 'row', axis=1, tiled=True)]
    all_to_all x0 -> x3, starting transfers between devices: none -> 22.2 us  [the longest x1 11.9 us: body(): lax.all_to_all(row_side, ('row', 'col'), split_axis=1, concat_axis=1, til...]
    another operation x0 -> x1, local copies, waits for them, and re-layouts: none -> 4 us  [body(): jnp.stack([row_received] * lax.axis_size('col'))]
  transfers between devices with their start and end apart: 2 -> 4, of which waited for: 1 -> 4; matrix products, arithmetic and copies ran while one was open for 9% -> 5% of each run, Pallas kernels for 0% -> 0%
where the time goes in v1:
time: 247 us; the launch traced here: 243 us
  waiting for transfers between devices  92.2 us (37%)
  matrix products  53.9 us (22%)
  local copies, waits for them, and re-layouts  48.9 us (20%)
  starting transfers between devices  22.4 us (9%)
  between operations  13.6 us (6%)
  other arithmetic  11.6 us (5%)
    all_to_all x1, waiting for transfers between devices, body(): lax.all_to_all(jnp.stack([row_received] * lax.axis_size('col')), 'col', 0...  48.9 us
    all_gather x1, waiting for transfers between devices, body(): column_panel = lax.all_gather(column_received, 'row', axis=1, tiled=True)  26.6 us
    dot_general x1, matrix products, body(): lax.dot_general(jnp.concatenate(lax.all_to_all(jnp.stack([row_received] *...  25.8 us
    dot_general x1, matrix products, transform(): jnp.einsum('gx,kxp->kgp', x_factor, product, precision=lax.Precision.HIGH...  13.6 us
    dot_general x4, matrix products, along_y(): jnp.einsum('hy,kgyz->kghz', factor_table, operand, precision=lax.Precisio...  12.3 us
    all_to_all x1, starting transfers between devices, body(): lax.all_to_all(row_side, ('row', 'col'), split_axis=1, concat_axis=1, til...  11.9 us
    gather x5, local copies, waits for them, and re-layouts, body(): density = jnp.take(sticks, stick_perm, axis=1).reshape(CAP, NPW)  10.3 us
    all_to_all x1, waiting for transfers between devices, body(): lax.all_to_all(column_side, ('row', 'col'), split_axis=1, concat_axis=1,...  9.52 us
  transfers between devices with their start and end apart: 4, of which 4 were waited for; matrix products, arithmetic and copies ran while one was open for 5% of the time, Pallas kernels for 0%

profile of v1, /device:TPU:1, one launch (start us, length us, event | category | flops | bytes accessed | tf_op | source)
XLA Modules:
  0.0 242.7 jit_solution(5360992580952839506)
XLA Ops:
  6.5 1.4 compare_and_fusion.2
  13.0 4.0 %gather_fusion.1 = bf16[4,96,9216]{2,1,0:T(8,128)(2,1)} fusion(bf16[2,96,9216]{2,1,0:T(8,128)(2,1)S(1)} %copy-done, s32[1024]{0:T(1024)} %pad_clamp_fusion.2), kind=kCustom, calls=%fused_computation.clone | custom fusion | bytes 14155792 | tf_op jit(solution)/shard_map/jit(_take)/gather | solution.py:68
  17.0 6.1 %gather_fusion.2 = bf16[4,96,9216]{2,1,0:T(8,128)(2,1)} fusion(bf16[2,96,9216]{2,1,0:T(8,128)(2,1)} %param.13, s32[1024]{0:T(1024)} %pad_clamp_fusion.1), kind=kCustom, calls=%fused_computation.2.clone | custom fusion | bytes 14155792 | tf_op jit(solution)/shard_map/jit(_take)/gather | solution.py:69
  23.1 13.6 %fusion.4 = f32[4,20,9216]{2,1,0:T(8,128)} fusion(bf16[4,96,9216]{2,1,0:T(8,128)(2,1)} %gather_fusion.2, bf16[4,96,9216]{2,1,0:T(8,128)(2,1)} %gather_fusion.1, pred[4]{0:T(512)(128)(4,1)} %get-tuple-element.9, pred[4]{0:T(512)(128)(4,1)} %get-tuple-element.10, f32[10,96]{1,0:T(8,128)S(1)} %get-tuple-element.8, f32[10,96]{1,0:T(8,128)S(1)} %get-tuple-element.6), kind=kOutput, calls=%fused_computation.9 | convolution fusion | flops 867043200 | bytes 17112584 | tf_op jit(solution)/shard_map/gx,kxp->kgp/dot_general | solution.py:27
  36.7 4.3 %reshape.120 = f32[4,20,96,96]{3,2,1,0:T(8,128)} reshape(f32[4,20,9216]{2,1,0:T(8,128)} %fusion.4) | data formatting | bytes 5898240 | tf_op jit(solution)/shard_map/reshape | solution.py:28
  41.0 3.4 %fusion.53 = f32[4,10,96,16]{2,3,1,0:T(8,128)} fusion(f32[4,20,96,96]{3,2,1,0:T(8,128)} %reshape.120), kind=kOutput, calls=%fused_computation.62 | convolution fusion | flops 70792704 | bytes 3194880 | tf_op jit(solution)/shard_map/hy,kgyz->kghz/dot_general | solution.py:35
  44.5 3.4 %fusion.51 = f32[4,10,96,16]{2,3,1,0:T(8,128)} fusion(f32[4,20,96,96]{3,2,1,0:T(8,128)} %reshape.120), kind=kOutput, calls=%fused_computation.60 | convolution fusion | flops 70792704 | bytes 3194880 | tf_op jit(solution)/shard_map/hy,kgyz->kghz/dot_general | solution.py:35
  51.3 1.5 broadcast_in_dim.46
  52.8 1.5 copy.48
  54.3 2.7 %fusion.13 = f32[4,10,16,96]{3,2,1,0:T(8,128)S(1)} fusion(f32[4,10,96,16]{2,3,1,0:T(8,128)} %fusion.53, f32[4,20,96,96]{3,2,1,0:T(8,128)} %reshape.120), kind=kOutput, calls=%fused_computation.20 | convolution fusion | flops 70854144 | bytes 3440640 | tf_op jit(solution)/shard_map/hy,kgyz->kghz/dot_general | solution.py:35
  57.6 2.7 %fusion.12 = f32[4,10,16,96]{3,2,1,0:T(8,128)S(1)} fusion(f32[4,10,96,16]{2,3,1,0:T(8,128)} %fusion.51, f32[4,20,96,96]{3,2,1,0:T(8,128)} %reshape.120), kind=kOutput, calls=%fused_computation.18 | convolution fusion | flops 70854144 | bytes 3440640 | tf_op jit(solution)/shard_map/hy,kgyz->kghz/dot_general | solution.py:35
  63.4 2.5 %gather_fusion = f32[160,4,128]{2,1,0:T(4,128)} fusion(f32[4,160,128]{2,0,1:T(4,128)} %maximum_multiply_fusion, s32[1024]{0:T(1024)S(1)} %pad_clamp_fusion), kind=kCustom, calls=%fused_computation.4 | custom fusion | bytes 656000 | tf_op jit(solution)/shard_map/jit(_take)/gather | solution.py:72
  65.9 1.7 copy.54
  67.7 2.0 gather.15
  69.7 2.0 copy.55
  74.2 1.8 select_multiply_fusion
  76.0 2.0 copy.56
  78.0 11.9 %all-to-all-start = ((f32[4,128,160]{2,0,1:T(4,128)}), f32[4,128,160]{2,0,1:T(4,128)}, u32[]{:S(2)}, u32[]{:S(2)}) async-start(f32[4,128,160]{2,0,1:T(4,128)} %copy.56), calls=%async_computation | async-start | bytes 1048576 | tf_op jit(solution)/shard_map/all_to_all | solution.py:86
  89.9 1.5 broadcast_in_dim.51
  91.4 2.0 gather.16
  95.8 7.2 %all-to-all-done = f32[4,128,160]{2,0,1:T(4,128)} async-done(((f32[4,128,160]{2,0,1:T(4,128)}), f32[4,128,160]{2,0,1:T(4,128)}, u32[]{:S(2)}, u32[]{:S(2)}) %all-to-all-start) | async-done | bytes 327712 | tf_op jit(solution)/shard_map/all_to_all | solution.py:86
  103.0 5.7 %all-to-all-start.2 = ((f32[4,128,160]{2,0,1:T(4,128)}), f32[4,128,160]{2,0,1:T(4,128)}, u32[]{:S(2)}, u32[]{:S(2)}) async-start(f32[4,128,160]{2,0,1:T(4,128)} %copy.60), calls=%async_computation.2 | async-start | bytes 1048576 | tf_op jit(solution)/shard_map/all_to_all | solution.py:87
  108.7 2.0 copy.57
  110.6 1.7 copy.72
  112.4 9.5 %all-to-all-done.2 = f32[4,128,160]{2,0,1:T(4,128)} async-done(((f32[4,128,160]{2,0,1:T(4,128)}), f32[4,128,160]{2,0,1:T(4,128)}, u32[]{:S(2)}, u32[]{:S(2)}) %all-to-all-start.2) | async-done | bytes 327712 | tf_op jit(solution)/shard_map/all_to_all | solution.py:87
  121.9 4.0 %stack.3 = f32[16,512,160]{1,2,0:T(8,128)} broadcast(f32[512,160]{0,1:T(8,128)} %bitcast.88), dimensions={1,2} | broadcast | bytes 5570560 | tf_op jit(solution)/shard_map/stack | solution.py:94
  125.9 4.6 %all-to-all-start.1 = ((f32[16,512,160]{1,2,0:T(8,128)}), f32[16,512,160]{1,2,0:T(8,128)}, u32[]{:S(2)}, u32[]{:S(2)}) async-start(f32[16,512,160]{1,2,0:T(8,128)} %stack.3), calls=%async_computation.1 | async-start | bytes 10485760 | tf_op jit(solution)/shard_map/all_to_all | solution.py:94
  130.7 2.0 copy.61
  132.7 1.8 copy.71
  134.5 26.6 %all-gather.2.cloned.1.call-done = f32[512,1280]{0,1:T(8,128)} async-done(((f32[512,160]{0,1:T(8,128)}), f32[512,1280]{0,1:T(8,128)}) %all-gather.2.cloned.1.call-update) | async-done | bytes 2621456 | tf_op jit(solution)/shard_map/all_gather | solution.py:91
  161.1 48.9 %all-to-all-done.1 = f32[16,512,160]{1,2,0:T(8,128)} async-done(((f32[16,512,160]{1,2,0:T(8,128)}), f32[16,512,160]{1,2,0:T(8,128)}, u32[]{:S(2)}, u32[]{:S(2)}) %all-to-all-start.1) | async-done | bytes 5242912 | tf_op jit(solution)/shard_map/all_to_all | solution.py:94
  210.0 25.8 %fusion.106 = f32[2560,1280]{1,0:T(8,128)} fusion(f32[512,2560]{0,1:T(8,128)} %bitcast.23, f32[512,1280]{0,1:T(8,128)} %all-gather.2.cloned.1.call-done), kind=kOutput, calls=%fused_computation.122 | convolution fusion | flops 20132659200 | bytes 20971520 | tf_op jit(solution)/shard_map/dot_general | solution.py:92
  (38 shorter events, 17.4 us)
Async XLA Ops:
  6.5 6.5 %copy-start = (bf16[2,96,9216]{2,1,0:T(8,128)(2,1)S(1)}, bf16[2,96,9216]{2,1,0:T(8,128)(2,1)}, u32[]{:S(2)}) copy-start(bf16[2,96,9216]{2,1,0:T(8,128)(2,1)} %param.12) | copy-start | bytes 10616836
  36.7 11.2 %copy-start.3 = (s32[160]{0:T(256)S(1)}, s32[160]{0:T(256)}, u32[]{:S(2)}) copy-start(s32[160]{0:T(256)} %compare_select_fusion) | copy-start | bytes 1924
  36.7 11.2 %copy-start.1 = (f32[2]{0:T(128)S(1)}, f32[2]{0:T(128)}, u32[]{:S(2)}) copy-start(f32[2]{0:T(128)} %param.15) | copy-start | bytes 28
  36.7 12.0 %copy-start.2 = (f32[2]{0:T(128)S(1)}, f32[2]{0:T(128)}, u32[]{:S(2)}) copy-start(f32[2]{0:T(128)} %param.14) | copy-start | bytes 28
  57.5 15.3 %copy-start.4 = (s32[1,4]{1,0:T(1,128)S(1)}, s32[1,4]{1,0:T(1,128)}, u32[]{:S(2)}) copy-start(s32[1,4]{1,0:T(1,128)} %param.17) | copy-start | bytes 52
  57.5 15.3 %copy-start.5 = (s32[1,4]{1,0:T(1,128)S(1)}, s32[1,4]{1,0:T(1,128)}, u32[]{:S(2)}) copy-start(s32[1,4]{1,0:T(1,128)} %param.16) | copy-start | bytes 52
  78.0 25.0 %all-to-all-start = ((f32[4,128,160]{2,0,1:T(4,128)}), f32[4,128,160]{2,0,1:T(4,128)}, u32[]{:S(2)}, u32[]{:S(2)}) async-start(f32[4,128,160]{2,0,1:T(4,128)} %copy.56), calls=%async_computation | async-start | bytes 1048576 | tf_op jit(solution)/shard_map/all_to_all | solution.py:86
  103.0 18.9 %all-to-all-start.2 = ((f32[4,128,160]{2,0,1:T(4,128)}), f32[4,128,160]{2,0,1:T(4,128)}, u32[]{:S(2)}, u32[]{:S(2)}) async-start(f32[4,128,160]{2,0,1:T(4,128)} %copy.60), calls=%async_computation.2 | async-start | bytes 1048576 | tf_op jit(solution)/shard_map/all_to_all | solution.py:87
  125.9 84.1 %all-to-all-start.1 = ((f32[16,512,160]{1,2,0:T(8,128)}), f32[16,512,160]{1,2,0:T(8,128)}, u32[]{:S(2)}, u32[]{:S(2)}) async-start(f32[16,512,160]{1,2,0:T(8,128)} %stack.3), calls=%async_computation.1 | async-start | bytes 10485760 | tf_op jit(solution)/shard_map/all_to_all | solution.py:94
  130.5 30.6 %all-gather.2.cloned.1.call-start = ((), (), s32[]{:S(2)}) async-start(), calls=%async_computation.3 | async-start | bytes 2949120 | tf_op jit(solution)/shard_map/all_gather | solution.py:91
Sparse Core Ops, SparseCore 0:
  134.6 26.4 all-gather.1
